TPU v7x, 32 devices: a whole 2x2x4 slice. The times are simulated.
32 devices in a mesh: batch: 8 (over z, x), tensor: 4 (over y, core).
Axes of the slice: x: 2, y: 2, z: 4, core: 2. Of those that a mesh axis runs over, the one named last changes fastest.
Arguments:
- tokens: bfloat16 [2, 8192, 768], P(None, 'batch'), may hold values from -6 to 6
- lengths: int32 [2, 8, 1024], P(None, 'batch'), may hold values from 0 to 512, as said below
- quarters: int32 [2], replicated, may hold values from 1 to 4, as said below
- query_weight: bfloat16 [768, 768], P(None, 'tensor'), may hold values from -0.3125 to 0.3125
- query_bias: float32 [768], P('tensor'), may hold values from -4 to 4
- key_weight: bfloat16 [768, 768], P(None, 'tensor'), may hold values from -0.3125 to 0.3125
- value_weight: bfloat16 [768, 768], P(None, 'tensor'), may hold values from -0.21875 to 0.21875
- value_bias: float32 [768], P('tensor'), may hold values from -6 to 6
- out_weight: bfloat16 [768, 768], P('tensor'), may hold values from -0.625 to 0.625
- out_bias: float32 [768], replicated, may hold values from -6 to 6
- norm1_gain: float32 [768], replicated, may hold values from 0.5 to 1.5
- norm1_shift: float32 [768], replicated, may hold values from -4 to 4
- in_weight: bfloat16 [768, 3072], P(None, 'tensor'), may hold values from -0.21875 to 0.21875
- in_bias: float32 [3072], P('tensor'), may hold values from -6 to 6
- down_weight: bfloat16 [3072, 768], P('tensor'), may hold values from -0.109375 to 0.109375
- down_bias: float32 [768], replicated, may hold values from -6 to 6
- norm2_gain: float32 [768], replicated, may hold values from 0.5 to 1.5
- norm2_shift: float32 [768], replicated, may hold values from -4 to 4
- cotangent: bfloat16 [2, 8192, 768], P(None, 'batch'), may hold values from -6 to 6
Outputs:
- layer_out: bfloat16 [2, 8192, 768], P(None, ('batch', 'tensor'))
- input_grad: float32 [2, 8192, 768], P(None, ('batch', 'tensor'))
- query_weight_grad: float32 [768, 768], P(None, 'tensor')
- query_bias_grad: float32 [768], P('tensor')
- key_weight_grad: float32 [768, 768], P(None, 'tensor')
- value_weight_grad: float32 [768, 768], P(None, 'tensor')
- value_bias_grad: float32 [768], P('tensor')
- out_weight_grad: float32 [768, 768], P('tensor')
- out_bias_grad: float32 [768], replicated
- norm1_gain_grad: float32 [768], replicated
- norm1_shift_grad: float32 [768], replicated
- in_weight_grad: float32 [768, 3072], P(None, 'tensor')
- in_bias_grad: float32 [3072], P('tensor')
- down_weight_grad: float32 [3072, 768], P('tensor')
- down_bias_grad: float32 [768], replicated
- norm2_gain_grad: float32 [768], replicated
- norm2_shift_grad: float32 [768], replicated
Inputs may be any that keep to these rules, and one draw needn't show every extreme that they name: Row lengths[m, b] lists, in order, the lengths of the sequences packed into block b of micro-batch m; they sum to 1024, and 0 marks an unused slot. In every micro-batch one block holds a sequence of exactly 512 tokens. Micro-batch m keeps the first 12 * quarters[m] / 4 heads and the first 3072 * quarters[m] / 4 units; exactly one micro-batch has quarters 4.
All inputs are finite; a program needn't handle non-finite values.
Results may differ from a plain program's by a relative error of at most 0.013.
The roundings to bfloat16 on the way count: a program that leaves them out, or rounds other values in their place, can miss the bound.
Values may be sent and summed in bfloat16 or wider, within the bound.
A program may use at most 128 MiB of HBM per device.

v0:
```python
import jax
import jax.numpy as jnp
from jax import lax
from jax.sharding import PartitionSpec as P

HEADS = 12
HEAD_DIM = 64
FF = 3072
EPSILON = 1e-12
ROOT_HALF = 0.7071067811865476
DENSITY_SCALE = 0.3989422804014327


def layer_norm(values_in, gain, shift):
    row_mean = jnp.mean(values_in, axis=-1, keepdims=True)
    centred = values_in - row_mean
    inverse = lax.rsqrt(jnp.mean(centred * centred, axis=-1, keepdims=True) + EPSILON)
    normed = centred * inverse
    return (normed * gain + shift, normed, inverse)


def norm_back(grad_in, normed, inverse, gain):
    spread = grad_in * gain
    return inverse * (
        spread
        - jnp.mean(spread, axis=-1, keepdims=True)
        - normed * jnp.mean(spread * normed, axis=-1, keepdims=True)
    )


def gelu_slope(values_in):
    return (
        0.5 * (1.0 + lax.erf(values_in * ROOT_HALF))
        + values_in * jnp.exp(-0.5 * values_in * values_in) * DENSITY_SCALE
    )


def segment_of(slot_lengths):
    ends_at = jnp.cumsum(slot_lengths)
    places = jnp.arange(slot_lengths.shape[0], dtype=jnp.int32)
    return jnp.sum((ends_at[None, :] <= places[:, None]).astype(jnp.int32), axis=1)


def rows_of(array_in, row_first, row_share):
    return lax.dynamic_slice_in_dim(array_in, row_first, row_share, 0)


def cross_dot(left, right):
    return lax.dot_general(
        left, right, (((0,), (0,)), ((), ())), preferred_element_type=jnp.float32
    )


def back_dot(left, weight_in):
    return lax.dot_general(
        left, weight_in, (((1,), (1,)), ((), ())), preferred_element_type=jnp.float32
    )


def block_scores(query_block, key_heads, segment_block, segment):
    scores = (
        jnp.einsum("qhd,khd->hqk", query_block, key_heads, preferred_element_type=jnp.float32)
        * 0.125
    )
    return jnp.where((segment_block[:, None] == segment[None, :])[None], scores, -1e30)


def attend(queries, key_heads, value_heads, segment, block_rows):
    row_count, head_count, head_width = queries.shape
    block_count = row_count // block_rows

    def one_block(block_index):
        block_start = block_index * block_rows
        query_block = lax.dynamic_slice_in_dim(queries, block_start, block_rows, 0)
        segment_block = lax.dynamic_slice_in_dim(segment, block_start, block_rows, 0)
        scores = block_scores(query_block, key_heads, segment_block, segment)
        top_score = jnp.max(scores, axis=-1, keepdims=True)
        expo = jnp.exp(scores - top_score)
        totals = jnp.sum(expo, axis=-1, keepdims=True)
        probs_low = (expo / totals).astype(jnp.bfloat16)
        context = jnp.einsum(
            "hqk,khd->qhd", probs_low, value_heads, preferred_element_type=jnp.float32
        )
        return (context, (top_score + jnp.log(totals))[..., 0])

    context, log_total = lax.map(one_block, jnp.arange(block_count))
    return (context.reshape(row_count, head_count, head_width), log_total)


def attend_back(queries, key_heads, value_heads, segment, log_total, grad_context, block_rows):
    row_count, head_count, head_width = queries.shape
    block_count = row_count // block_rows

    def one_block(totals_in, block_index):
        key_total, value_total = totals_in
        block_start = block_index * block_rows
        query_block = lax.dynamic_slice_in_dim(queries, block_start, block_rows, 0)
        segment_block = lax.dynamic_slice_in_dim(segment, block_start, block_rows, 0)
        grad_block = lax.dynamic_slice_in_dim(grad_context, block_start, block_rows, 0)
        scores = block_scores(query_block, key_heads, segment_block, segment)
        probs = jnp.exp(scores - log_total[block_index][:, :, None])
        value_total = value_total + jnp.einsum(
            "hqk,qhd->khd",
            probs.astype(jnp.bfloat16),
            grad_block,
            preferred_element_type=jnp.float32,
        )
        grad_probs = jnp.einsum(
            "qhd,khd->hqk", grad_block, value_heads, preferred_element_type=jnp.float32
        )
        grad_scores = (
            probs * (grad_probs - jnp.sum(probs * grad_probs, axis=-1, keepdims=True))
        ).astype(jnp.bfloat16)
        query_grad = (
            jnp.einsum("hqk,khd->qhd", grad_scores, key_heads, preferred_element_type=jnp.float32)
            * 0.125
        )
        key_total = (
            key_total
            + jnp.einsum(
                "hqk,qhd->khd", grad_scores, query_block, preferred_element_type=jnp.float32
            )
            * 0.125
        )
        return ((key_total, value_total), query_grad)

    empty_grads = jnp.zeros((row_count, head_count, head_width), jnp.float32)
    (key_grad, value_grad), query_grads = lax.scan(
        one_block, (empty_grads, empty_grads), jnp.arange(block_count)
    )
    return (query_grads.reshape(row_count, head_count, head_width), key_grad, value_grad)


def local(
    tokens,
    lengths,
    quarters,
    query_weight,
    query_bias,
    key_weight,
    value_weight,
    value_bias,
    out_weight,
    out_bias,
    norm1_gain,
    norm1_shift,
    in_weight,
    in_bias,
    down_weight,
    down_bias,
    norm2_gain,
    norm2_shift,
    cotangent,
):
    group_count = lax.axis_size("tensor")
    tensor_place = lax.axis_index("tensor")
    micro_count, row_count, model_width = tokens.shape
    row_share = row_count // group_count
    row_first = tensor_place * row_share
    local_heads = query_weight.shape[1] // HEAD_DIM
    local_units = in_weight.shape[1]
    head_ids = tensor_place * local_heads + jnp.arange(local_heads, dtype=jnp.int32)
    unit_ids = tensor_place * local_units + jnp.arange(local_units, dtype=jnp.int32)
    block_rows = min(512, row_count)
    outputs = []
    input_grads = []
    split_terms = None
    shared_terms = None
    for micro_step in range(micro_count):
        live_quarter = quarters[micro_step]
        head_live = (4 * head_ids < HEADS * live_quarter).astype(jnp.float32)
        unit_live = (4 * unit_ids < FF * live_quarter).astype(jnp.float32)
        inputs = tokens[micro_step]
        segment = segment_of(lengths[micro_step, 0])
        queries = (
            jnp.dot(inputs, query_weight, preferred_element_type=jnp.float32) + query_bias
        ).astype(jnp.bfloat16)
        queries = queries.reshape(row_count, local_heads, HEAD_DIM)
        key_heads = jnp.dot(inputs, key_weight, preferred_element_type=jnp.float32).astype(
            jnp.bfloat16
        )
        key_heads = key_heads.reshape(row_count, local_heads, HEAD_DIM)
        value_heads = (
            jnp.dot(inputs, value_weight, preferred_element_type=jnp.float32) + value_bias
        ).astype(jnp.bfloat16)
        value_heads = value_heads.reshape(row_count, local_heads, HEAD_DIM)
        context, log_total = attend(queries, key_heads, value_heads, segment, block_rows)
        context_low = (
            (context * head_live[None, :, None])
            .astype(jnp.bfloat16)
            .reshape(row_count, local_heads * HEAD_DIM)
        )
        attn_partial = jnp.dot(context_low, out_weight, preferred_element_type=jnp.float32)
        inputs_wide = inputs.astype(jnp.float32)
        grad_out = cotangent[micro_step].astype(jnp.float32)
        grad_out_rows = rows_of(grad_out, row_first, row_share)
        attended = lax.psum(attn_partial, "tensor")
        hidden, normed_one, inverse_one = layer_norm(
            inputs_wide + attended + out_bias, norm1_gain, norm1_shift
        )
        hidden_low = hidden.astype(jnp.bfloat16)
        pre_act = jnp.dot(hidden_low, in_weight, preferred_element_type=jnp.float32) + in_bias
        active_low = (jax.nn.gelu(pre_act, approximate=False) * unit_live).astype(jnp.bfloat16)
        ffn_partial = jnp.dot(active_low, down_weight, preferred_element_type=jnp.float32)
        mixed = lax.psum(ffn_partial, "tensor")
        result_full, normed_two, inverse_two = layer_norm(
            hidden + mixed + down_bias, norm2_gain, norm2_shift
        )
        result_rows = rows_of(result_full, row_first, row_share)
        grad_mid2 = norm_back(grad_out, normed_two, inverse_two, norm2_gain)
        grad_mid2_rows = rows_of(grad_mid2, row_first, row_share)
        normed_two_rows = rows_of(normed_two, row_first, row_share)
        grad_mid2_low = grad_mid2.astype(jnp.bfloat16)
        outputs.append(result_rows.astype(jnp.bfloat16))
        norm2_gain_term = jnp.sum(grad_out_rows * normed_two_rows, axis=0)
        norm2_shift_term = jnp.sum(grad_out_rows, axis=0)
        down_bias_term = jnp.sum(grad_mid2_rows, axis=0)
        down_term = cross_dot(active_low, grad_mid2_low)
        grad_active = back_dot(grad_mid2_low, down_weight)
        grad_pre_low = (grad_active * unit_live * gelu_slope(pre_act)).astype(jnp.bfloat16)
        in_bias_term = jnp.sum(grad_pre_low.astype(jnp.float32), axis=0)
        in_term = cross_dot(hidden_low, grad_pre_low)
        hidden_partial = back_dot(grad_pre_low, in_weight)
        grad_hidden = grad_mid2 + lax.psum(hidden_partial, "tensor")
        grad_mid1 = norm_back(grad_hidden, normed_one, inverse_one, norm1_gain)
        grad_hidden_rows = rows_of(grad_hidden, row_first, row_share)
        normed_one_rows = rows_of(normed_one, row_first, row_share)
        grad_mid1_rows = rows_of(grad_mid1, row_first, row_share)
        grad_mid1_low = grad_mid1.astype(jnp.bfloat16)
        norm1_gain_term = jnp.sum(grad_hidden_rows * normed_one_rows, axis=0)
        norm1_shift_term = jnp.sum(grad_hidden_rows, axis=0)
        out_bias_term = jnp.sum(grad_mid1_rows, axis=0)
        out_term = cross_dot(context_low, grad_mid1_low)
        grad_context_low = (
            back_dot(grad_mid1_low, out_weight)
            .astype(jnp.bfloat16)
            .reshape(row_count, local_heads, HEAD_DIM)
        )
        grad_context_low = grad_context_low * head_live.astype(jnp.bfloat16)[None, :, None]
        grad_queries, grad_keys, grad_values = attend_back(
            queries, key_heads, value_heads, segment, log_total, grad_context_low, block_rows
        )
        grad_queries_low = grad_queries.astype(jnp.bfloat16).reshape(
            row_count, local_heads * HEAD_DIM
        )
        grad_keys_low = grad_keys.astype(jnp.bfloat16).reshape(row_count, local_heads * HEAD_DIM)
        grad_values_low = grad_values.astype(jnp.bfloat16).reshape(
            row_count, local_heads * HEAD_DIM
        )
        query_term = cross_dot(inputs, grad_queries_low)
        query_bias_term = jnp.sum(grad_queries_low.astype(jnp.float32), axis=0)
        key_term = cross_dot(inputs, grad_keys_low)
        value_term = cross_dot(inputs, grad_values_low)
        value_bias_term = jnp.sum(grad_values_low.astype(jnp.float32), axis=0)
        input_partial = (
            back_dot(grad_queries_low, query_weight)
            + back_dot(grad_keys_low, key_weight)
            + back_dot(grad_values_low, value_weight)
        )
        input_rows = (
            lax.psum_scatter(
                input_partial.astype(jnp.bfloat16), "tensor", scatter_dimension=0, tiled=True
            ).astype(jnp.float32)
            + grad_mid1_rows
        )
        input_grads.append(input_rows)
        new_split = (
            query_term,
            query_bias_term,
            key_term,
            value_term,
            value_bias_term,
            out_term,
            in_term,
            in_bias_term,
            down_term,
        )
        new_shared = (
            out_bias_term,
            norm1_gain_term,
            norm1_shift_term,
            down_bias_term,
            norm2_gain_term,
            norm2_shift_term,
        )
        if micro_step == 0:
            split_terms = new_split
            shared_terms = new_shared
        else:
            split_terms = jax.tree.map(jnp.add, split_terms, new_split)
            shared_terms = jax.tree.map(jnp.add, shared_terms, new_shared)
    (
        query_acc,
        query_bias_acc,
        key_acc,
        value_acc,
        value_bias_acc,
        out_acc,
        in_acc,
        in_bias_acc,
        down_acc,
    ) = split_terms
    (
        out_bias_acc,
        norm1_gain_acc,
        norm1_shift_acc,
        down_bias_acc,
        norm2_gain_acc,
        norm2_shift_acc,
    ) = shared_terms
    (
        query_sum,
        query_bias_sum,
        key_sum,
        value_sum,
        value_bias_sum,
        out_sum,
        in_sum,
        in_bias_sum,
        down_sum,
    ) = lax.psum(
        (
            query_acc,
            query_bias_acc,
            key_acc,
            value_acc,
            value_bias_acc,
            out_acc,
            in_acc,
            in_bias_acc,
            down_acc,
        ),
        "batch",
    )
    (
        out_bias_sum,
        norm1_gain_sum,
        norm1_shift_sum,
        down_bias_sum,
        norm2_gain_sum,
        norm2_shift_sum,
    ) = lax.psum(
        (
            out_bias_acc,
            norm1_gain_acc,
            norm1_shift_acc,
            down_bias_acc,
            norm2_gain_acc,
            norm2_shift_acc,
        ),
        ("batch", "tensor"),
    )
    return (
        jnp.stack(outputs),
        jnp.stack(input_grads),
        query_sum,
        query_bias_sum,
        key_sum,
        value_sum,
        value_bias_sum,
        out_sum,
        out_bias_sum,
        norm1_gain_sum,
        norm1_shift_sum,
        in_sum,
        in_bias_sum,
        down_sum,
        down_bias_sum,
        norm2_gain_sum,
        norm2_shift_sum,
    )


def solution(mesh):
    in_specs = (
        P(None, "batch", None),
        P(None, "batch", None),
        P(),
        P(None, "tensor"),
        P("tensor"),
        P(None, "tensor"),
        P(None, "tensor"),
        P("tensor"),
        P("tensor", None),
        P(),
        P(),
        P(),
        P(None, "tensor"),
        P("tensor"),
        P("tensor", None),
        P(),
        P(),
        P(),
        P(None, "batch", None),
    )
    out_specs = (
        P(None, ("batch", "tensor"), None),
        P(None, ("batch", "tensor"), None),
        P(None, "tensor"),
        P("tensor"),
        P(None, "tensor"),
        P(None, "tensor"),
        P("tensor"),
        P("tensor", None),
        P(),
        P(),
        P(),
        P(None, "tensor"),
        P("tensor"),
        P("tensor", None),
        P(),
        P(),
        P(),
    )
    return jax.shard_map(local, mesh=mesh, in_specs=in_specs, out_specs=out_specs, check_vma=False)
```

profile of v0, /device:TPU:0, one launch (start us, length us, event | category | flops | bytes accessed | tf_op | source)
XLA Modules:
  0.0 904.1 jit_solution(4392460739010797551)
XLA Ops:
  7.3 2.3 fusion.147
  22.5 35.8 %while.54 = (s32[]{:T(128)}, f32[2,512,3,64]{1,0,3,2:T(2,128)}, f32[2,3,512]{2,1,0:T(4,128)}, s32[2]{0:T(128)}, s32[1024]{0:T(1024)S(1)}, /*index=5*/bf16[1024,3...) while((s32[]{:T(128)}, f32[2,512,3,64]{1,0,3,2:T(2,128)}, ...), condition=%wide.region_6.7_spmd, body=%wide.region_3.6_spmd.sunk | while | flops 422050304 | bytes 23982280 | solution.py:86
  28.3 3.1 fusion.333
  32.4 8.1 dynamic_update_slice.33
  46.0 3.1 fusion.333
  50.2 8.1 dynamic_update_slice.33
  58.3 2.5 copy.82
  63.0 32.8 %while.55 = (s32[]{:T(128)}, f32[2,512,3,64]{1,0,3,2:T(2,128)}, f32[2,3,512]{2,1,0:T(4,128)}, s32[2]{0:T(128)}, s32[1024]{0:T(1024)S(1)}, /*index=5*/bf16[1024,3...) while((s32[]{:T(128)}, f32[2,512,3,64]{1,0,3,2:T(2,128)}, ...), condition=%wide.region_19.20_spmd, body=%wide.region_16.19_spmd.sunk | while | flops 422050304 | bytes 24084736 | solution.py:86
  68.5 2.3 fusion.338
  71.3 8.1 dynamic_update_slice.35
  84.9 2.3 fusion.338
  87.6 8.1 dynamic_update_slice.35
  98.4 3.3 fusion.220
  101.7 2.4 fusion.219
  106.0 120.6 %all-reduce.17.cloned.1.call-done = (f32[1024,768]{1,0:T(8,128)}, f32[1024,768]{1,0:T(8,128)}) async-done(((f32[1024,768]{1,0:T(8,128)}, f32[1024,768]{1,0:T(8,128)}), (f32[1024,768]{1,0:T(8,128)}, f32[1024,768]{1,0:T(8,128)})) %all-reduce.17.cloned.1.call-update) | async-done | bytes 6291472 | tf_op jit(solution)/shard_map/psum | solution.py:197
  226.6 4.8 fusion.180
  239.0 15.7 %fusion.73 = (bf16[1024,768]{1,0:T(8,128)(2,1)S(1)}, bf16[1024,768]{1,0:T(8,128)(2,1)S(1)}, f32[1024,768]{1,0:T(8,128)}) fusion(f32[768]{0:T(1024)S(1)} %fusion.217, f32[768]{0:T(1024)S(1)} %copy-done.86, f32[768]{0:T(1024)S(1)} %fusion.218, f32[1024,768]{1,0:T(8,128)S(1)} %fusion.195, bf16[768,768]{1,0:T(8,128)(2,1)S(1)} %copy-done, ...), kind=kOutput, calls=%fused_computation.95 | convolution fusion | flops 1315700736 | bytes 13777920 | tf_op jit(solution)/shard_map/dot_general | solution.py:202
  254.7 3.1 fusion.227
  257.8 3.1 fusion.228
  261.1 119.8 %all-reduce.15.cloned.1.call-done = (f32[1024,768]{1,0:T(8,128)}, f32[1024,768]{1,0:T(8,128)}) async-done(((f32[1024,768]{1,0:T(8,128)}, f32[1024,768]{1,0:T(8,128)}), (f32[1024,768]{1,0:T(8,128)}, f32[1024,768]{1,0:T(8,128)})) %all-reduce.15.cloned.1.call-update) | async-done | bytes 6291472 | tf_op jit(solution)/shard_map/psum | solution.py:205
  380.8 5.8 fusion.224
  388.6 2.4 fusion.106
  394.2 2.3 copy-done.93
  396.6 3.0 convert_reduce_fusion.2
  399.6 3.1 fusion.232
  402.7 3.0 convert_reduce_fusion.3
  406.9 3.2 fusion.229
  410.2 4.0 fusion.191
  414.2 2.9 convolution_add_fusion
  417.1 112.9 %all-reduce.13.cloned.1.call-done = (f32[1024,768]{1,0:T(8,128)}, f32[1024,768]{1,0:T(8,128)}) async-done(((f32[1024,768]{1,0:T(8,128)}, f32[1024,768]{1,0:T(8,128)}), (f32[1024,768]{1,0:T(8,128)}, f32[1024,768]{1,0:T(8,128)})) %all-reduce.13.cloned.1.call-update) | async-done | bytes 6291472 | tf_op jit(solution)/shard_map/psum | solution.py:224
  530.0 9.6 %multiply_reduce_fusion.11 = (f32[1024]{0:T(1024)S(1)}, f32[1024]{0:T(1024)S(1)}, f32[1024]{0:T(1024)S(1)}, f32[1024]{0:T(1024)S(1)}, f32[1024,768]{1,0:T(8,128)}, /*index=5*/f32[1024,768]{1,0:T(8,128)}) fusion(f32[768]{0:T(1024)S(1)} %copy-done.68, f32[1024,768]{1,0:T(8,128)} %copy-done.9, f32[1024,768]{1,0:T(8,128)} %copy-done.10, ...), kind=kLoop, calls=%fused_computation.175 | loop fusion | flops 7860224 | bytes 25185280 | tf_op jit(solution)/shard_map/reduce_sum | solution.py:26
  539.6 6.9 subtract_multiply_fusion.2
  549.2 29.8 %while.56 = (s32[]{:T(128)}, f32[1024,3,64]{0,2,1:T(8,128)S(1)}, f32[1024,3,64]{0,2,1:T(8,128)}, bf16[2,512,3,64]{1,3,2,0:T(8,128)(2,1)S(1)}, s32[2]{0:T(128)S(1...) while((s32[]{:T(128)}, f32[1024,3,64]{0,2,1:T(8,128)S(1)}, ...), condition=%wide.region_33.34_spmd.clone, body=%wide.region_31.33_spmd.clone.sunk | while | flops 1031830016 | bytes 61137236 | solution.py:128
  556.6 3.8 multiply_reduce_fusion.16
  571.5 3.8 multiply_reduce_fusion.16
  579.8 3.3 convolution_convert_fusion
  588.6 26.4 %while.57 = (s32[]{:T(128)}, f32[1024,3,64]{0,2,1:T(8,128)S(1)}, f32[1024,3,64]{0,2,1:T(8,128)}, bf16[2,512,3,64]{1,3,2,0:T(8,128)(2,1)}, s32[2]{0:T(128)S(1)}, ...) while((s32[]{:T(128)}, f32[1024,3,64]{0,2,1:T(8,128)S(1)}, ...), condition=%wide.region_42.43_spmd.clone, body=%wide.region_40.42_spmd.clone.sunk | while | flops 1031830016 | bytes 64283020 | solution.py:128
  595.8 2.5 multiply_reduce_fusion.17
  606.8 2.0 fusion.363
  608.8 2.5 multiply_reduce_fusion.17
  620.2 4.0 fusion.197
  624.2 3.0 convolution_add_fusion.1
  635.3 2.6 slice_convert_fusion
  642.7 2.0 dynamic-slice_reduce_fusion.4
  644.8 22.2 %all-reduce.1 = (f32[192]{0:T(256)}, f32[192]{0:T(256)}, f32[768]{0:T(1024)}) all-reduce(f32[192]{0:T(256)S(1)} %add.459, f32[192]{0:T(256)S(1)} %add.465, f32[768]{0:T(1024)S(1)} %add.471), channel_id=1, replica_groups=mesh['batch'=8,'tensor'=4] {'batch'}, use_global_device_ids=true, to_apply=%region_47.48 | all-reduce | flops 1152 | bytes 9216 | tf_op jit(solution)/shard_map/psum | solution.py:321
  669.7 40.9 %all-reduce = (f32[768]{0:T(1024)}, f32[768]{0:T(1024)}, f32[768]{0:T(1024)}, f32[768]{0:T(1024)}, f32[768]{0:T(1024)}, /*index=5*/f32[768]{0:T(1024)}) all-reduce(f32[768]{0:T(1024)S(1)} %add.467, f32[768]{0:T(1024)S(1)} %add.468, f32[768]{0:T(1024)S(1)} %add.469, ...), channel_id=1, replica_groups=mesh['batch'=8,'tensor'=4] {'batch','tensor'}, use_global_device_ids=true, to_apply=%region_56.57 | all-reduce | flops 4608 | bytes 36864 | tf_op jit(solution)/shard_map/psum | solution.py:342
  711.8 175.7 %all-reduce.11.cloned.1.call-done = (f32[768,192]{0,1:T(8,128)}, f32[768,192]{0,1:T(8,128)}, f32[768,192]{0,1:T(8,128)}, f32[192,768]{1,0:T(8,128)}, f32[768,768]{1,0:T(8,128)}, /*index=5*/f32[768,768]{1,0:T(8,128)}) async-done(((f32[768,192]{0,1:T(8,128)}, f32[768,192]{0,1:T(8,128)}, f32[768,192]{0,1:T(8,128)}, f32[192,768]{1,0:T(8,128)}, f32[768,768]{1,0:T(8,128)}, /*index=5*/f32[768,768]{1,0:T(8,128)}), ...) | async-done | bytes 7077904 | tf_op jit(solution)/shard_map/psum | solution.py:321
  887.6 2.1 copy.150
  (400 shorter events, 121.7 us)
Async XLA Ops:
  7.2 229.2 %copy-start = (bf16[768,768]{1,0:T(8,128)(2,1)S(1)}, bf16[768,768]{1,0:T(8,128)(2,1)}, u32[]{:S(2)}) copy-start(bf16[768,768]{1,0:T(8,128)(2,1)} %param.39) | copy-start | bytes 3538948
  7.2 219.4 %all-reduce.17.cloned.1.call-start = ((), (), s32[]{:S(2)}) async-start(), calls=%async_computation.7 | async-start | bytes 12582912 | tf_op jit(solution)/shard_map/psum | solution.py:197
  7.3 4.1 copy-start.43
  7.3 4.1 copy-start.88
  13.5 4.6 copy-start.74
  18.0 83.7 %copy-start.70 = (f32[192]{0:T(256)}, f32[192]{0:T(256)S(1)}, u32[]{:S(2)}) copy-start(f32[192]{0:T(256)S(1)} %mul.438) | copy-start | bytes 2308
  18.1 79.4 %copy-start.72 = (f32[192]{0:T(256)}, f32[192]{0:T(256)S(1)}, u32[]{:S(2)}) copy-start(f32[192]{0:T(256)S(1)} %mul.464) | copy-start | bytes 2308
  58.3 4.7 copy-start.4
  58.3 4.7 copy-start.20
  58.3 4.7 copy-start.53
  70.8 8.5 copy-start.63
  87.2 8.5 copy-start.63
  95.7 8.4 copy-start.2
  95.7 8.4 copy-start.18
  95.7 8.4 copy-start.27
  95.7 8.3 copy-start.51
  95.7 5.9 copy-start.29
  95.8 5.9 copy-start.33
  104.1 122.5 %copy-start.65 = (f32[768]{0:T(1024)S(1)}, f32[768]{0:T(1024)}, u32[]{:S(2)}) copy-start(f32[768]{0:T(1024)} %param.36) | copy-start | bytes 9220
  104.1 276.7 %all-reduce.15.cloned.1.call-start = ((), (), s32[]{:S(2)}) async-start(), calls=%async_computation.6 | async-start | bytes 12582912 | tf_op jit(solution)/shard_map/psum | solution.py:205
  226.6 4.8 copy-start.7
  226.6 5.6 copy-start.15
  226.6 6.5 copy-start.16
  238.0 16.7 %copy-start.92 = (f32[1024,768]{1,0:T(8,128)}, f32[1024,768]{1,0:T(8,128)S(1)}, u32[]{:S(2)}) copy-start(f32[1024,768]{1,0:T(8,128)S(1)} %fusion.195) | copy-start | bytes 9437188
  239.0 15.7 %copy-start.84 = (bf16[768,768]{1,0:T(8,128)(2,1)S(1)}, bf16[768,768]{1,0:T(8,128)(2,1)}, u32[]{:S(2)}) copy-start(bf16[768,768]{1,0:T(8,128)(2,1)} %param.41) | copy-start | bytes 3538948
  260.8 120.0 %copy-start.75 = (f32[768]{0:T(1024)S(1)}, f32[768]{0:T(1024)}, u32[]{:S(2)}) copy-start(f32[768]{0:T(1024)} %param.42) | copy-start | bytes 9220
  260.9 269.1 %all-reduce.13.cloned.1.call-start = ((), (), s32[]{:S(2)}) async-start(), calls=%async_computation.5 | async-start | bytes 12582912 | tf_op jit(solution)/shard_map/psum | solution.py:224
  391.1 5.5 copy-start.93
  394.2 5.4 copy-start.22
  394.2 8.5 copy-start.24
  410.1 256.9 %reduce-scatter.3.cloned.1.call-start = ((), (), s32[]{:S(2)}) async-start(), calls=%async_computation.2 | async-start | bytes 1966080 | tf_op jit(solution)/shard_map/reduce_scatter | solution.py:261
  410.1 4.0 copy-start.23
  410.1 4.0 copy-start.91
  571.5 3.8 copy-start.59
  579.0 4.1 copy-start.60
  579.1 4.2 copy-start.34
  579.1 4.2 copy-start.47
  584.7 3.9 copy-start.3
  584.7 3.8 copy-start.19
  584.7 3.8 copy-start.28
  584.8 3.8 copy-start.52
  584.8 3.8 copy-start.64
  586.6 81.7 %reduce-scatter.5.cloned.1.call-start = ((), (), s32[]{:S(2)}) async-start(), calls=%async_computation.3 | async-start | bytes 1966080 | tf_op jit(solution)/shard_map/reduce_scatter | solution.py:261
  619.9 267.6 %all-reduce.11.cloned.1.call-start = ((), (), s32[]{:S(2)}) async-start(), calls=%async_computation.4 | async-start | bytes 14155776 | tf_op jit(solution)/shard_map/psum | solution.py:321
  620.2 4.0 copy-start.11
  620.2 4.0 copy-start.96
  887.6 5.9 copy-start.61
  887.6 6.7 copy-start.42
  (64 other events, 136.4 us)
Sparse Core Ops, SparseCore 0:
  104.2 122.3 all-reduce.16
  261.0 119.8 all-reduce.14
  410.2 119.7 all-reduce.12
  586.7 28.2 reduce-scatter.2
  620.1 28.3 reduce-scatter.4
  654.5 232.9 all-reduce.10
where the time goes:
time: 911 us; the launch traced here: 904 us
  waiting for transfers between devices  529 us (58%)
  matrix products  128 us (14%)
  local copies, waits for them, and re-layouts  78.6 us (9%)
  other arithmetic  71.7 us (8%)
  blocking collectives  63 us (7%)
  between operations  18.2 us (2%)
  loops' own time  14.2 us (2%)
    psum x1, waiting for transfers between devices, local(): lax.psum((query_acc, query_bias_acc, key_acc, value_acc, value_bias_acc,...  176 us
    psum x1, waiting for transfers between devices, local(): attended = lax.psum(attn_partial, 'tensor')  121 us
    psum x1, waiting for transfers between devices, local(): mixed = lax.psum(ffn_partial, 'tensor')  120 us
    psum x1, waiting for transfers between devices, local(): grad_hidden = grad_mid2 + lax.psum(hidden_partial, 'tensor')  113 us
    psum x1, blocking collectives, local(): lax.psum((out_bias_acc, norm1_gain_acc, norm1_shift_acc, down_bias_acc, n...  40.9 us
    dynamic_update_slice x8, local copies, waits for them, and re-layouts, attend(): context, log_total = lax.map(one_block, jnp.arange(block_count))  33.9 us
    unnamed x190, local copies, waits for them, and re-layouts  26.4 us
    dot_general x12, matrix products, back_dot(): lax.dot_general(left, weight_in, (((1,), (1,)), ((), ())), preferred_elem...  22.4 us
  transfers between devices with their start and end apart: 6, of which 4 were waited for; matrix products, arithmetic and copies ran while one was open for 7% of the time, Pallas kernels for 0%

commit v1 on v0

--- a/solution.py
+++ b/solution.py
@@ -221,7 +221,7 @@
         in_bias_term = jnp.sum(grad_pre_low.astype(jnp.float32), axis=0)
         in_term = cross_dot(hidden_low, grad_pre_low)
         hidden_partial = back_dot(grad_pre_low, in_weight)
-        grad_hidden = grad_mid2 + lax.psum(hidden_partial, "tensor")
+        grad_hidden = grad_mid2 + jnp.sum(lax.all_gather(hidden_partial, axis_name="tensor"), 0)
         grad_mid1 = norm_back(grad_hidden, normed_one, inverse_one, norm1_gain)
         grad_hidden_rows = rows_of(grad_hidden, row_first, row_share)
         normed_one_rows = rows_of(normed_one, row_first, row_share)

time: 911 us -> 958 us (1.052)
  waiting for transfers between devices: 529 us -> 555 us
  other arithmetic: 71.7 us -> 88 us
    all_gather x0 -> x2, waiting for transfers between devices: none -> 139 us  [local(): lax.all_gather(hidden_partial, axis_name='tensor')]
    psum x1 -> x0, waiting for transfers between devices: 113 us -> none  [local(): grad_hidden = grad_mid2 + lax.psum(hidden_partial, 'tensor')]
    reduce_sum x0 -> x2, other arithmetic: none -> 14.9 us  [local(): jnp.sum(lax.all_gather(hidden_partial, axis_name='tensor'), 0)]
    unnamed x190 -> x186, local copies, waits for them, and re-layouts: 26.4 us -> 27.2 us
  transfers between devices with their start and end apart: 6 -> 7, of which waited for: 4 -> 5; matrix products, arithmetic and copies ran while one was open for 7% -> 8% of each run, Pallas kernels for 0% -> 0%
where the time goes in v1:
time: 958 us; the launch traced here: 951 us
  waiting for transfers between devices  555 us (58%)
  matrix products  132 us (14%)
  other arithmetic  88 us (9%)
  local copies, waits for them, and re-layouts  79.5 us (8%)
  blocking collectives  62.8 us (7%)
  between operations  18.2 us (2%)
  loops' own time  14 us (1%)
    psum x1, waiting for transfers between devices, local(): lax.psum((query_acc, query_bias_acc, key_acc, value_acc, value_bias_acc,...  176 us
    all_gather x2, waiting for transfers between devices, local(): lax.all_gather(hidden_partial, axis_name='tensor')  139 us
    psum x1, waiting for transfers between devices, local(): attended = lax.psum(attn_partial, 'tensor')  121 us
    psum x1, waiting for transfers between devices, local(): mixed = lax.psum(ffn_partial, 'tensor')  120 us
    psum x1, blocking collectives, local(): lax.psum((out_bias_acc, norm1_gain_acc, norm1_shift_acc, down_bias_acc, n...  40.6 us
    dynamic_update_slice x8, local copies, waits for them, and re-layouts, attend(): context, log_total = lax.map(one_block, jnp.arange(block_count))  33.9 us
    unnamed x186, local copies, waits for them, and re-layouts  27.2 us
    dot_general x12, matrix products, back_dot(): lax.dot_general(left, weight_in, (((1,), (1,)), ((), ())), preferred_elem...  25.4 us
  transfers between devices with their start and end apart: 7, of which 5 were waited for; matrix products, arithmetic and copies ran while one was open for 8% of the time, Pallas kernels for 0%

profile of v1, /device:TPU:0, one launch (start us, length us, event | category | flops | bytes accessed | tf_op | source)
XLA Modules:
  0.0 951.1 jit_solution(3184664620574709415)
XLA Ops:
  7.3 2.3 fusion.147
  22.5 35.8 %while.54 = (s32[]{:T(128)}, f32[2,512,3,64]{1,0,3,2:T(2,128)}, f32[2,3,512]{2,1,0:T(4,128)}, s32[2]{0:T(128)}, s32[1024]{0:T(1024)S(1)}, /*index=5*/bf16[1024,3...) while((s32[]{:T(128)}, f32[2,512,3,64]{1,0,3,2:T(2,128)}, ...), condition=%wide.region_6.7_spmd, body=%wide.region_3.6_spmd.sunk | while | flops 422050304 | bytes 23982280 | solution.py:86
  28.3 3.1 fusion.333
  32.4 8.1 dynamic_update_slice.33
  46.0 3.1 fusion.333
  50.2 8.1 dynamic_update_slice.33
  58.3 2.5 copy.84
  62.9 32.7 %while.55 = (s32[]{:T(128)}, f32[2,512,3,64]{1,0,3,2:T(2,128)}, f32[2,3,512]{2,1,0:T(4,128)}, s32[2]{0:T(128)}, s32[1024]{0:T(1024)S(1)}, /*index=5*/bf16[1024,3...) while((s32[]{:T(128)}, f32[2,512,3,64]{1,0,3,2:T(2,128)}, ...), condition=%wide.region_19.20_spmd, body=%wide.region_16.19_spmd.sunk | while | flops 422050304 | bytes 24084736 | solution.py:86
  68.5 2.3 fusion.338
  71.2 8.1 dynamic_update_slice.35
  84.8 2.3 fusion.338
  87.6 8.1 dynamic_update_slice.35
  98.3 3.3 fusion.220
  101.6 2.4 fusion.219
  106.0 120.6 %all-reduce.13.cloned.1.call-done = (f32[1024,768]{1,0:T(8,128)}, f32[1024,768]{1,0:T(8,128)}) async-done(((f32[1024,768]{1,0:T(8,128)}, f32[1024,768]{1,0:T(8,128)}), (f32[1024,768]{1,0:T(8,128)}, f32[1024,768]{1,0:T(8,128)})) %all-reduce.13.cloned.1.call-update) | async-done | bytes 6291472 | tf_op jit(solution)/shard_map/psum | solution.py:197
  226.6 4.8 fusion.180
  239.0 15.7 %fusion.73 = (bf16[1024,768]{1,0:T(8,128)(2,1)S(1)}, bf16[1024,768]{1,0:T(8,128)(2,1)S(1)}, f32[1024,768]{1,0:T(8,128)}) fusion(f32[768]{0:T(1024)S(1)} %fusion.217, f32[768]{0:T(1024)S(1)} %copy-done.85, f32[768]{0:T(1024)S(1)} %fusion.218, f32[1024,768]{1,0:T(8,128)S(1)} %fusion.195, bf16[768,768]{1,0:T(8,128)(2,1)S(1)} %copy-done, ...), kind=kOutput, calls=%fused_computation.95 | convolution fusion | flops 1315700736 | bytes 13777920 | tf_op jit(solution)/shard_map/dot_general | solution.py:202
  254.7 3.1 fusion.227
  257.8 3.1 fusion.228
  261.1 119.7 %all-reduce.11.cloned.1.call-done = (f32[1024,768]{1,0:T(8,128)}, f32[1024,768]{1,0:T(8,128)}) async-done(((f32[1024,768]{1,0:T(8,128)}, f32[1024,768]{1,0:T(8,128)}), (f32[1024,768]{1,0:T(8,128)}, f32[1024,768]{1,0:T(8,128)})) %all-reduce.11.cloned.1.call-update) | async-done | bytes 6291472 | tf_op jit(solution)/shard_map/psum | solution.py:205
  380.8 5.8 fusion.224
  388.6 2.4 fusion.106
  391.1 3.1 subtract_multiply_fusion.1
  396.5 3.1 convert_reduce_fusion.2
  400.7 3.0 fusion.232
  403.9 6.1 convert_reduce_fusion.3
  411.1 3.1 fusion.229
  414.6 4.8 fusion.191
  420.4 2.9 convolution_add_fusion
  423.3 63.0 %all-gather.7.cloned.1.call-done = f32[4096,768]{1,0:T(8,128)} async-done(((f32[1024,768]{1,0:T(8,128)}), f32[4096,768]{1,0:T(8,128)}) %all-gather.7.cloned.1.call-update) | async-done | bytes 12582928 | tf_op jit(solution)/shard_map/all_gather | solution.py:224
  486.2 7.4 reduce_sum.395
  493.7 76.1 %all-gather.5.cloned.1.call-done = f32[4096,768]{1,0:T(8,128)} async-done(((f32[1024,768]{1,0:T(8,128)}), f32[4096,768]{1,0:T(8,128)}) %all-gather.5.cloned.1.call-update) | async-done | bytes 12582928 | tf_op jit(solution)/shard_map/all_gather | solution.py:224
  569.8 7.5 reduce_sum.390
  577.3 9.5 multiply_reduce_fusion.11
  586.8 7.1 subtract_multiply_fusion.2
  596.4 29.8 %while.56 = (s32[]{:T(128)}, f32[1024,3,64]{0,2,1:T(8,128)S(1)}, f32[1024,3,64]{0,2,1:T(8,128)}, bf16[2,512,3,64]{1,3,2,0:T(8,128)(2,1)S(1)}, s32[2]{0:T(128)S(1...) while((s32[]{:T(128)}, f32[1024,3,64]{0,2,1:T(8,128)S(1)}, ...), condition=%wide.region_33.34_spmd.clone, body=%wide.region_31.33_spmd.clone.sunk | while | flops 1031830016 | bytes 61137236 | solution.py:128
  603.9 3.8 multiply_reduce_fusion.16
  618.8 3.8 multiply_reduce_fusion.16
  627.1 3.3 convolution_convert_fusion
  635.8 26.2 %while.57 = (s32[]{:T(128)}, f32[1024,3,64]{0,2,1:T(8,128)S(1)}, f32[1024,3,64]{0,2,1:T(8,128)}, bf16[2,512,3,64]{1,3,2,0:T(8,128)(2,1)}, s32[2]{0:T(128)S(1)}, ...) while((s32[]{:T(128)}, f32[1024,3,64]{0,2,1:T(8,128)S(1)}, ...), condition=%wide.region_42.43_spmd.clone, body=%wide.region_40.42_spmd.clone.sunk | while | flops 1031830016 | bytes 64283020 | solution.py:128
  642.8 2.5 multiply_reduce_fusion.17
  655.8 2.5 multiply_reduce_fusion.17
  667.2 4.0 fusion.197
  671.2 3.0 convolution_add_fusion.1
  682.4 2.6 slice_convert_fusion
  691.9 22.2 %all-reduce.1 = (f32[192]{0:T(256)}, f32[192]{0:T(256)}, f32[768]{0:T(1024)}) all-reduce(f32[192]{0:T(256)S(1)} %add.455, f32[192]{0:T(256)S(1)} %add.461, f32[768]{0:T(1024)S(1)} %add.467), channel_id=1, replica_groups=mesh['batch'=8,'tensor'=4] {'batch'}, use_global_device_ids=true, to_apply=%region_47.48 | all-reduce | flops 1152 | bytes 9216 | tf_op jit(solution)/shard_map/psum | solution.py:321
  716.9 40.6 %all-reduce = (f32[768]{0:T(1024)}, f32[768]{0:T(1024)}, f32[768]{0:T(1024)}, f32[768]{0:T(1024)}, f32[768]{0:T(1024)}, /*index=5*/f32[768]{0:T(1024)}) all-reduce(f32[768]{0:T(1024)S(1)} %add.463, f32[768]{0:T(1024)S(1)} %add.464, f32[768]{0:T(1024)S(1)} %add.465, ...), channel_id=1, replica_groups=mesh['batch'=8,'tensor'=4] {'batch','tensor'}, use_global_device_ids=true, to_apply=%region_56.57 | all-reduce | flops 4608 | bytes 36864 | tf_op jit(solution)/shard_map/psum | solution.py:342
  758.7 175.8 %all-reduce.9.cloned.1.call-done = (f32[768,192]{0,1:T(8,128)}, f32[768,192]{0,1:T(8,128)}, f32[768,192]{0,1:T(8,128)}, f32[192,768]{1,0:T(8,128)}, f32[768,768]{1,0:T(8,128)}, /*index=5*/f32[768,768]{1,0:T(8,128)}) async-done(((f32[768,192]{0,1:T(8,128)}, f32[768,192]{0,1:T(8,128)}, f32[768,192]{0,1:T(8,128)}, f32[192,768]{1,0:T(8,128)}, f32[768,768]{1,0:T(8,128)}, /*index=5*/f32[768,768]{1,0:T(8,128)}), ...) | async-done | bytes 7077904 | tf_op jit(solution)/shard_map/psum | solution.py:321
  (401 shorter events, 129.4 us)
Async XLA Ops:
  7.2 229.1 %copy-start = (bf16[768,768]{1,0:T(8,128)(2,1)S(1)}, bf16[768,768]{1,0:T(8,128)(2,1)}, u32[]{:S(2)}) copy-start(bf16[768,768]{1,0:T(8,128)(2,1)} %param.39) | copy-start | bytes 3538948
  7.2 219.4 %all-reduce.13.cloned.1.call-start = ((), (), s32[]{:S(2)}) async-start(), calls=%async_computation.8 | async-start | bytes 12582912 | tf_op jit(solution)/shard_map/psum | solution.py:197
  7.3 4.1 copy-start.42
  7.3 4.1 copy-start.87
  13.5 4.6 copy-start.73
  18.0 83.7 %copy-start.69 = (f32[192]{0:T(256)}, f32[192]{0:T(256)S(1)}, u32[]{:S(2)}) copy-start(f32[192]{0:T(256)S(1)} %mul.438) | copy-start | bytes 2308
  18.1 79.3 %copy-start.71 = (f32[192]{0:T(256)}, f32[192]{0:T(256)S(1)}, u32[]{:S(2)}) copy-start(f32[192]{0:T(256)S(1)} %mul.464) | copy-start | bytes 2308
  58.3 4.7 copy-start.4
  58.3 4.7 copy-start.20
  58.3 4.7 copy-start.52
  70.8 8.5 copy-start.62
  87.2 8.5 copy-start.62
  95.7 8.4 copy-start.2
  95.7 8.4 copy-start.18
  95.7 8.4 copy-start.26
  95.7 8.3 copy-start.50
  95.7 5.9 copy-start.28
  95.7 5.9 copy-start.32
  104.1 122.5 %copy-start.64 = (f32[768]{0:T(1024)S(1)}, f32[768]{0:T(1024)}, u32[]{:S(2)}) copy-start(f32[768]{0:T(1024)} %param.36) | copy-start | bytes 9220
  104.1 276.7 %all-reduce.11.cloned.1.call-start = ((), (), s32[]{:S(2)}) async-start(), calls=%async_computation.7 | async-start | bytes 12582912 | tf_op jit(solution)/shard_map/psum | solution.py:205
  226.6 4.8 copy-start.7
  226.6 5.6 copy-start.15
  226.6 6.5 copy-start.16
  238.1 16.6 %copy-start.91 = (f32[1024,768]{1,0:T(8,128)}, f32[1024,768]{1,0:T(8,128)S(1)}, u32[]{:S(2)}) copy-start(f32[1024,768]{1,0:T(8,128)S(1)} %fusion.195) | copy-start | bytes 9437188
  239.0 15.7 %copy-start.83 = (bf16[768,768]{1,0:T(8,128)(2,1)S(1)}, bf16[768,768]{1,0:T(8,128)(2,1)}, u32[]{:S(2)}) copy-start(bf16[768,768]{1,0:T(8,128)(2,1)} %param.41) | copy-start | bytes 3538948
  260.8 120.0 %copy-start.74 = (f32[768]{0:T(1024)S(1)}, f32[768]{0:T(1024)}, u32[]{:S(2)}) copy-start(f32[768]{0:T(1024)} %param.42) | copy-start | bytes 9220
  260.9 225.4 %all-gather.7.cloned.1.call-start = ((), (), s32[]{:S(2)}) async-start(), calls=%async_computation.5 | async-start | bytes 15728640 | tf_op jit(solution)/shard_map/all_gather | solution.py:224
  391.1 4.6 copy-start.25
  391.1 4.6 copy-start.84
  391.1 5.4 copy-start.92
  395.7 3.9 copy-start.22
  403.8 166.0 %all-gather.5.cloned.1.call-start = ((), (), s32[]{:S(2)}) async-start(), calls=%async_computation.4 | async-start | bytes 15728640 | tf_op jit(solution)/shard_map/all_gather | solution.py:224
  414.3 299.8 %reduce-scatter.3.cloned.1.call-start = ((), (), s32[]{:S(2)}) async-start(), calls=%async_computation.2 | async-start | bytes 1966080 | tf_op jit(solution)/shard_map/reduce_scatter | solution.py:261
  414.6 4.9 copy-start.23
  414.6 5.8 copy-start.90
  626.3 4.1 copy-start.59
  626.3 4.2 copy-start.33
  626.3 4.2 copy-start.46
  632.0 3.8 copy-start.3
  632.0 3.8 copy-start.19
  632.0 3.8 copy-start.27
  632.0 3.8 copy-start.51
  633.8 81.7 %reduce-scatter.5.cloned.1.call-start = ((), (), s32[]{:S(2)}) async-start(), calls=%async_computation.3 | async-start | bytes 1966080 | tf_op jit(solution)/shard_map/reduce_scatter | solution.py:261
  666.9 267.6 %all-reduce.9.cloned.1.call-start = ((), (), s32[]{:S(2)}) async-start(), calls=%async_computation.6 | async-start | bytes 14155776 | tf_op jit(solution)/shard_map/psum | solution.py:321
  667.2 4.0 copy-start.11
  667.2 4.0 copy-start.95
  934.5 5.9 copy-start.60
  934.5 6.7 copy-start.41
  (63 other events, 134.1 us)
Sparse Core Ops, SparseCore 0:
  104.2 122.3 all-reduce.12
  261.0 119.7 all-reduce.10
  403.9 82.2 all-gather.6
  487.7 82.0 all-gather.4
  634.0 28.0 reduce-scatter.2
  667.0 28.1 reduce-scatter.4
  701.5 232.9 all-reduce.8
